TPU v7x, 32 devices: a whole 2x2x4 slice. The times are simulated.
32 devices in a mesh: group: 2 (over x), tensor: 8 (over z, y), dp: 2 (over core).
Axes of the slice: x: 2, y: 2, z: 4, core: 2. Of those that a mesh axis runs over, the one named last changes fastest.
Arguments:
- features: bfloat16 [512, 8192], P(('group', 'dp'), 'tensor'), parts along dimension 0, may hold values from -64 to 64
- cotangent: bfloat16 [512, 8192], P(('group', 'dp'), 'tensor'), parts along dimension 0, may hold values from -64 to 64
- token_tenant: int32 [512], P(('group', 'dp')), parts along dimension 0, may hold values from 0 to 15
- owner_device: int32 [32], P('group'), parts along dimension 0, may hold values from 0 to 15, each once
- frozen_weight: bfloat16 [8192, 8192], P('tensor'), may hold values from -0.09375 to 0.09375
- adapter_down: bfloat16 [32, 16, 8192], P('group', None, 'tensor'), parts along dimension 0, may hold values from -0.0625 to 0.0625
- adapter_up: bfloat16 [32, 16, 8192], P('group', None, 'tensor'), parts along dimension 0, may hold values from -0.29882812 to 0.29882812
- momentum_down: float32 [32, 16, 8192], P(('group', 'tensor', 'dp')), parts along dimension 0, may hold values from -12 to 12
- momentum_up: float32 [32, 16, 8192], P(('group', 'tensor', 'dp')), parts along dimension 0, may hold values from -3 to 3
- variance_down: float32 [32, 16, 8192], P(('group', 'tensor', 'dp')), parts along dimension 0, may hold values from 0.3 to 3
- variance_up: float32 [32, 16, 8192], P(('group', 'tensor', 'dp')), parts along dimension 0, may hold values from 0.02 to 0.2
Outputs:
- projected: bfloat16 [512, 8192], P(('group', 'dp'), 'tensor'), parts along dimension 0
- updated_down: bfloat16 [32, 16, 8192], P('group', None, 'tensor'), parts along dimension 0
- updated_up: bfloat16 [32, 16, 8192], P('group', None, 'tensor'), parts along dimension 0
- mean_down: float32 [32, 16, 8192], P(('group', 'tensor', 'dp')), parts along dimension 0
- mean_up: float32 [32, 16, 8192], P(('group', 'tensor', 'dp')), parts along dimension 0
- power_down: float32 [32, 16, 8192], P(('group', 'tensor', 'dp')), parts along dimension 0
- power_up: float32 [32, 16, 8192], P(('group', 'tensor', 'dp')), parts along dimension 0
There are 2 independent parts, one for each index of `group`. A program takes and returns all parts, laid end to end along the dimension named above; an argument that names none is the same for every part. Nothing has to cross between parts.
Inputs may be any that keep to these rules, and one draw needn't show every extreme that they name: Tenant t belongs to the device whose index along tensor+dp (dp fastest) is owner_device[t]; every index appears once.
All inputs are finite; a program needn't handle non-finite values.
Results may differ from a plain program's by a relative error of at most 0.0014.
The roundings to bfloat16 on the way count: a program that leaves them out, or rounds other values in their place, can miss the bound.
Values sent between devices are 32-bit elements; how exact they have to be, the bound alone decides.
A program may use at most 128 MiB of HBM per device.

v0:
```python
import functools

import jax
import jax.numpy as jnp
from jax import lax
from jax.experimental import pallas as pl
from jax.experimental.pallas import tpu as pltpu
from jax.sharding import PartitionSpec as P

MESH = pl.DeviceIdType.MESH

adapter_scale = 2.0
clip_norm = 12000.0
learn_rate = 0.004
beta_one = 0.9
beta_two = 0.999
adam_eps = 1e-08
correct_one = 1.0 - beta_one**20
correct_two = 1.0 - beta_two**20

CHUNKS = 2


def adam_step(gradient, factor, moment, square):
    clipped = gradient * factor
    moment_next = beta_one * moment + (1.0 - beta_one) * clipped
    square_next = beta_two * square + (1.0 - beta_two) * clipped * clipped
    change = (
        learn_rate * (moment_next / correct_one) / (jnp.sqrt(square_next / correct_two) + adam_eps)
    )
    return (moment_next, square_next, change)


def line_order(line):
    order = []
    for near in range((line + 1) // 2):
        order.append(line - 1 - near)
        if near != line - 1 - near:
            order.append(near)
    return order


def kernel(
    n,
    owner_ref,
    tenant_ref,
    feat_ref,
    cot_ref,
    down_ref,
    up_ref,
    weight_ref,
    mom_down_ref,
    mom_up_ref,
    var_down_ref,
    var_up_ref,
    proj_ref,
    new_down_ref,
    new_up_ref,
    mean_down_ref,
    mean_up_ref,
    power_down_ref,
    power_up_ref,
    wbuf,
    state,
    rpart,
    rbuf,
    gsend,
    grecv,
    summed,
    owned,
    change,
    changes,
    ysend,
    yrecv,
    part,
    going_up,
    going_down,
    adapted,
    wsem,
    msem,
    rank_s,
    rank_r,
    g_s,
    g_r,
    a_s,
    a_r,
    c_s,
    c_r,
    f_s,
    f_r,
    y_s,
    y_r,
    z_s,
    u_r,
    d_r,
):
    tenants, lowrank, w = down_ref.shape
    tokens, depth = feat_ref.shape
    line = n // 2
    order = line_order(line)
    t = lax.axis_index("tensor")
    d = lax.axis_index("dp")
    zi, yi = t // 2, lax.rem(t, 2)
    mate = {"dp": 1 - d}
    pair = {"tensor": zi * 2 + 1 - yi}

    quarter = max(1, line // 4)
    waves = (
        order[:quarter],
        order[quarter : 2 * quarter],
        order[2 * quarter : 3 * quarter],
        order[3 * quarter :],
    )
    height = tokens // CHUNKS
    paired = n & (n - 1) == 0

    def peer(o):
        return t ^ (n - o) if paired else lax.rem(t + o, n)

    def giver(o):
        return t ^ (n - o) if paired else lax.rem(t + n - o, n)

    def columns(block):
        return pl.ds(pl.multiple_of(block * w, w), w)

    barrier = pltpu.get_barrier_semaphore()

    @pl.loop(1, n)
    def _(o):
        pl.semaphore_signal(barrier, inc=1, device_id={"tensor": peer(o)}, device_id_type=MESH)

    pl.semaphore_signal(barrier, inc=1, device_id=mate, device_id_type=MESH)

    def weight_copy(i, block):
        return pltpu.make_async_copy(
            weight_ref.at[:, columns(block)], wbuf.at[i], wsem.at[i]
        )

    blocks = [z * 2 + 1 - yi for z in order] + [z * 2 + yi for z in order]
    for i, block in enumerate(blocks):
        weight_copy(i, block).start()
    state_copies = [
        pltpu.make_async_copy(ref, state.at[i], msem.at[i])
        for i, ref in enumerate((mom_down_ref, mom_up_ref, var_down_ref, var_up_ref))
    ]
    for copy in state_copies:
        copy.start()

    tenant = tenant_ref[...]
    contract = (((1,), (1,)), ((), ()))
    tenant_row = lax.broadcasted_iota(jnp.int32, (tenants, lowrank, tokens), 0)
    tenant_hit = tenant_row == tenant[None]

    def rank_part(adapter, rows):
        scores = lax.dot_general(
            adapter[...].reshape(tenants * lowrank, w),
            rows[...],
            contract,
            preferred_element_type=jnp.float32,
        ).reshape(tenants, lowrank, tokens)
        return jnp.sum(jnp.where(tenant_hit, scores, 0.0), axis=0)

    rpart[0] = rank_part(down_ref, feat_ref)
    rpart[1] = rank_part(up_ref, cot_ref)

    pl.semaphore_wait(barrier, n)

    def rank_copy(o, source):
        return pltpu.make_async_remote_copy(
            src_ref=rpart,
            dst_ref=rbuf.at[source],
            send_sem=rank_s.at[o],
            recv_sem=rank_r.at[source],
            device_id={"tensor": peer(o)},
            device_id_type=MESH,
        )

    @pl.loop(1, n)
    def _(o):
        rank_copy(o, t).start()

    def rows_of(c):
        return pl.ds(c * height, height)

    def pair_copy(z, c):
        return pltpu.make_async_remote_copy(
            src_ref=ysend.at[z, rows_of(c)],
            dst_ref=yrecv.at[z, rows_of(c)],
            send_sem=y_s.at[z * CHUNKS + c],
            recv_sem=y_r.at[z * CHUNKS + c],
            device_id=pair,
            device_id_type=MESH,
        )

    def pair_start(z):
        for c in range(CHUNKS):
            pair_copy(z, c).start()

    def frozen(i, block):
        weight_copy(i, block).wait()
        return jnp.dot(feat_ref[...], wbuf[i], preferred_element_type=jnp.float32)

    for i, z in enumerate(order):
        ysend[z] = frozen(i, blocks[i])
        if z in waves[0]:
            pair_start(z)

    slot = jnp.zeros_like(tenant)
    slot = lax.fori_loop(
        0, tenants, lambda k, s: jnp.where(tenant == k, owner_ref[k], s), slot
    )

    @pl.loop(1, n)
    def _(o):
        rank_copy(o, giver(o)).wait_recv()

    rbuf[t] = rpart[...]
    total = rbuf[0]
    for source in range(1, n):
        total = total + rbuf[source]
    low = adapter_scale * total
    down_low = low[0].astype(jnp.bfloat16).astype(jnp.float32)
    up_low = low[1].astype(jnp.bfloat16).astype(jnp.float32)

    half_row = lax.broadcasted_iota(jnp.int32, (n, lowrank, tokens), 0) * 2

    def half_grads(side):
        hit = half_row + side == slot[None]

        def one(values, rows):
            spread = jnp.where(hit, values[None], 0.0).reshape(n * lowrank, tokens)
            return jnp.dot(
                spread.astype(jnp.bfloat16), rows[...], preferred_element_type=jnp.float32
            ).reshape(n, lowrank, w)

        return one(up_low, feat_ref), one(down_low, cot_ref)

    def mate_copy(i):
        return pltpu.make_async_remote_copy(
            src_ref=gsend.at[i],
            dst_ref=grecv.at[i],
            send_sem=g_s.at[i],
            recv_sem=g_r.at[i],
            device_id=mate,
            device_id_type=MESH,
        )

    theirs = half_grads(1 - d)
    for i in range(2):
        gsend[i] = theirs[i]
    for i in range(2):
        mate_copy(i).start()
    mine = half_grads(d)
    for i in range(2):
        summed[:, i] = mine[i]
    for i in range(2):
        mate_copy(i).wait_recv()
        summed[:, i] = summed[:, i] + grecv[i]

    def grad_copy(o, source):
        return pltpu.make_async_remote_copy(
            src_ref=summed.at[peer(o)],
            dst_ref=owned.at[source],
            send_sem=a_s.at[o],
            recv_sem=a_r.at[source],
            device_id={"tensor": peer(o)},
            device_id_type=MESH,
        )

    @pl.loop(1, n)
    def _(o):
        grad_copy(o, t).start()

    for z in waves[1]:
        pair_start(z)

    owned[t] = summed[t]

    down_spread = jnp.where(tenant_hit, down_low[None], 0.0).reshape(tenants * lowrank, tokens)
    adapted[...] = jnp.dot(
        jnp.transpose(down_spread).astype(jnp.bfloat16),
        up_ref[...].reshape(tenants * lowrank, w),
        preferred_element_type=jnp.float32,
    )
    for i, z in enumerate(order):
        part[z] = frozen(line + i, blocks[line + i])

    def up_copy(z, c):
        return pltpu.make_async_remote_copy(
            src_ref=part.at[z, rows_of(c)],
            dst_ref=going_up.at[z, rows_of(c)],
            send_sem=z_s.at[z * CHUNKS + c],
            recv_sem=u_r.at[z * CHUNKS + c],
            device_id={"tensor": lax.rem(t + 2, n)},
            device_id_type=MESH,
        )

    def down_copy(z, c):
        return pltpu.make_async_remote_copy(
            src_ref=part.at[z, rows_of(c)],
            dst_ref=going_down.at[z, rows_of(c)],
            send_sem=z_s.at[z * CHUNKS + c],
            recv_sem=d_r.at[z * CHUNKS + c],
            device_id={"tensor": lax.rem(t + n - 2, n)},
            device_id_type=MESH,
        )

    def ends(z):
        for c in range(CHUNKS):
            at = rows_of(c)
            pair_copy(z, c).wait_recv()
            part[z, at] = part[z, at] + yrecv[z, at]

            @pl.when(jnp.logical_and(zi == 0, z > 0))
            def _():
                up_copy(z, c).start()

            @pl.when(jnp.logical_and(zi == line - 1, z < line - 1))
            def _():
                down_copy(z, c).start()

    def middles(z):
        for c in range(CHUNKS):
            at = rows_of(c)

            @pl.when(jnp.logical_and(zi > 0, zi < z))
            def _():
                up_copy(z, c).wait_recv()
                part[z, at] = part[z, at] + going_up[z, at]
                up_copy(z, c).start()

            @pl.when(jnp.logical_and(zi > z, zi < line - 1))
            def _():
                down_copy(z, c).wait_recv()
                part[z, at] = part[z, at] + going_down[z, at]
                down_copy(z, c).start()

    for z in waves[0]:
        ends(z)

    for copy in state_copies:
        copy.wait()

    @pl.loop(1, n)
    def _(o):
        grad_copy(o, giver(o)).wait_recv()

    for z in waves[2]:
        pair_start(z)

    def squares_of(k, acc):
        g = owned[k]
        return acc + jnp.sum(g * g, axis=0)

    squares = lax.fori_loop(0, n, squares_of, jnp.zeros((lowrank, w), jnp.float32))
    squares = jnp.sum(squares, axis=(0, 1), keepdims=True)
    factor = clip_norm / jnp.maximum(jnp.sqrt(squares), clip_norm)

    def change_copy(o, source):
        return pltpu.make_async_remote_copy(
            src_ref=change.at[peer(o)],
            dst_ref=changes.at[source * 2 + d],
            send_sem=c_s.at[o],
            recv_sem=c_r.at[source],
            device_id={"tensor": peer(o)},
            device_id_type=MESH,
        )

    def step_piece(k):
        at = columns(k)
        for i in range(2):
            mean, power, moved = adam_step(
                owned[k, i], factor, state[i, 0, :, at], state[2 + i, 0, :, at]
            )
            state[i, 0, :, at] = mean
            state[2 + i, 0, :, at] = power
            change[k, i] = moved

    @pl.loop(1, n)
    def _(o):
        step_piece(peer(o))

        @pl.when(o > 1)
        def _():
            change_copy(o - 1, t).start()

    step_piece(t)
    change_copy(n - 1, t).start()
    changes[t * 2 + d] = change[t]

    def forward_copy(source, side):
        at = source * 2 + side
        return pltpu.make_async_remote_copy(
            src_ref=changes.at[at],
            dst_ref=changes.at[at],
            send_sem=f_s.at[source],
            recv_sem=f_r.at[source],
            device_id=mate,
            device_id_type=MESH,
        )

    forward_copy(t, d).start()
    state_outs = [
        pltpu.make_async_copy(state.at[i], ref, msem.at[i])
        for i, ref in enumerate((mean_down_ref, mean_up_ref, power_down_ref, power_up_ref))
    ]
    for copy in state_outs:
        copy.start()

    for z in waves[3]:
        pair_start(z)
    for z in waves[1]:
        ends(z)
    for z in waves[0]:
        middles(z)
    for z in waves[2]:
        ends(z)

    @pl.loop(1, n)
    def _(o):
        change_copy(o, giver(o)).wait_recv()
        forward_copy(giver(o), d).start()

    for z in waves[3]:
        ends(z)
    for z in waves[1] + waves[2]:
        middles(z)

    @pl.loop(0, n)
    def _(source):
        forward_copy(source, 1 - d).wait_recv()

    @pl.loop(0, tenants)
    def _(k):
        back = changes[owner_ref[k]]
        new_down_ref[k] = (down_ref[k].astype(jnp.float32) - back[0]).astype(jnp.bfloat16)
        new_up_ref[k] = (up_ref[k].astype(jnp.float32) - back[1]).astype(jnp.bfloat16)

    for z in waves[3]:
        middles(z)

    for c in range(CHUNKS):
        at = rows_of(c)

        @pl.when(zi > 0)
        def _():
            up_copy(zi, c).wait_recv()
            part[zi, at] = part[zi, at] + going_up[zi, at]

        @pl.when(zi < line - 1)
        def _():
            down_copy(zi, c).wait_recv()
            part[zi, at] = part[zi, at] + going_down[zi, at]

        proj_ref[at] = (part[zi, at] + adapted[at]).astype(proj_ref.dtype)

    for copy in state_outs:
        copy.wait()

    @pl.loop(1, n)
    def _(o):
        rank_copy(o, t).wait_send()
        grad_copy(o, t).wait_send()
        change_copy(o, t).wait_send()

    @pl.loop(0, n)
    def _(source):
        forward_copy(source, d).wait_send()

    for i in range(2):
        mate_copy(i).wait_send()
    for z in order:
        for c in range(CHUNKS):
            pair_copy(z, c).wait_send()

            @pl.when(zi != z)
            def _():
                up_copy(z, c).wait_send()


def hand_out(*refs):
    count = len(refs) // 3
    sources, results, held = refs[:count], refs[count : 2 * count], refs[2 * count : 3 * count]
    sems = refs[-1]
    ins = [pltpu.make_async_copy(sources[i], held[i], sems.at[0, i]) for i in range(count)]
    outs = [pltpu.make_async_copy(held[i], results[i], sems.at[1, i]) for i in range(count)]
    for copy in ins:
        copy.start()
    for i in range(count):
        ins[i].wait()
        outs[i].start()
    for copy in outs:
        copy.wait()


def on_device(n, *args):
    (
        features,
        cotangent,
        token_tenant,
        owner_device,
        frozen_weight,
        adapter_down,
        adapter_up,
        momentum_down,
        momentum_up,
        variance_down,
        variance_up,
    ) = args
    tokens, depth = features.shape
    tenants, lowrank, w = adapter_down.shape
    line = n // 2
    f32 = jnp.float32
    vmem = pl.BlockSpec(memory_space=pltpu.VMEM)
    hbm = pl.BlockSpec(memory_space=pl.ANY)
    dma = pltpu.SemaphoreType.DMA
    shape = jax.ShapeDtypeStruct
    results = pl.pallas_call(
        functools.partial(kernel, n),
        out_shape=(
            shape((tokens, w), jnp.bfloat16),
            shape(adapter_down.shape, jnp.bfloat16),
            shape(adapter_up.shape, jnp.bfloat16),
            shape(momentum_down.shape, f32),
            shape(momentum_up.shape, f32),
            shape(variance_down.shape, f32),
            shape(variance_up.shape, f32),
        ),
        in_specs=[pl.BlockSpec(memory_space=pltpu.SMEM)] + [vmem] * 5 + [hbm] * 5,
        out_specs=[vmem] * 3 + [hbm] * 4,
        scratch_shapes=[
            pltpu.VMEM((n, depth, w), jnp.bfloat16),
            pltpu.VMEM((4,) + momentum_down.shape, f32),
            pltpu.VMEM((2, lowrank, tokens), f32),
            pltpu.VMEM((n, 2, lowrank, tokens), f32),
            pltpu.VMEM((2, n, lowrank, w), f32),
            pltpu.VMEM((2, n, lowrank, w), f32),
            pltpu.VMEM((n, 2, lowrank, w), f32),
            pltpu.VMEM((n, 2, lowrank, w), f32),
            pltpu.VMEM((n, 2, lowrank, w), f32),
            pltpu.VMEM((tenants, 2, lowrank, w), f32),
            pltpu.VMEM((line, tokens, w), f32),
            pltpu.VMEM((line, tokens, w), f32),
            pltpu.VMEM((line, tokens, w), f32),
            pltpu.VMEM((line, tokens, w), f32),
            pltpu.VMEM((line, tokens, w), f32),
            pltpu.VMEM((tokens, w), f32),
            dma((n,)),
            dma((4,)),
            dma((n,)),
            dma((n,)),
            dma((2,)),
            dma((2,)),
            dma((n,)),
            dma((n,)),
            dma((n,)),
            dma((n,)),
            dma((n,)),
            dma((n,)),
            dma((line * CHUNKS,)),
            dma((line * CHUNKS,)),
            dma((line * CHUNKS,)),
            dma((line * CHUNKS,)),
            dma((line * CHUNKS,)),
        ],
        compiler_params=pltpu.CompilerParams(
            collective_id=0, has_side_effects=True, vmem_limit_bytes=60 * 1024 * 1024
        ),
    )(
        owner_device,
        token_tenant.reshape(1, tokens),
        features,
        cotangent,
        adapter_down,
        adapter_up,
        frozen_weight,
        momentum_down,
        momentum_up,
        variance_down,
        variance_up,
    )
    return pl.pallas_call(
        hand_out,
        out_shape=tuple(shape(r.shape, r.dtype) for r in results),
        in_specs=[hbm] * len(results),
        out_specs=[hbm] * len(results),
        scratch_shapes=[pltpu.VMEM(r.shape, r.dtype) for r in results]
        + [dma((2, len(results)))],
    )(*results)


def solution(mesh):
    in_specs = (
        P(("group", "dp"), "tensor"),
        P(("group", "dp"), "tensor"),
        P(("group", "dp")),
        P("group"),
        P("tensor", None),
        P("group", None, "tensor"),
        P("group", None, "tensor"),
        P(("group", "tensor", "dp"), None, None),
        P(("group", "tensor", "dp"), None, None),
        P(("group", "tensor", "dp"), None, None),
        P(("group", "tensor", "dp"), None, None),
    )
    out_specs = (
        P(("group", "dp"), "tensor"),
        P("group", None, "tensor"),
        P("group", None, "tensor"),
        P(("group", "tensor", "dp"), None, None),
        P(("group", "tensor", "dp"), None, None),
        P(("group", "tensor", "dp"), None, None),
        P(("group", "tensor", "dp"), None, None),
    )
    return jax.shard_map(
        functools.partial(on_device, mesh.shape["tensor"]),
        mesh=mesh,
        in_specs=in_specs,
        out_specs=out_specs,
        check_vma=False,
    )
```

profile of v0, /device:TPU:9, one launch (start us, length us, event | category | flops | bytes accessed | tf_op | source)
XLA Modules:
  0.0 104.4 jit_solution(6545079835095044865)
XLA Ops:
  0.6 100.9 %shard_map.162 = (bf16[128,1024]{1,0:T(8,128)(2,1)}, bf16[16,16,1024]{2,1,0:T(8,128)(2,1)}, bf16[16,16,1024]{2,1,0:T(8,128)(2,1)}, f32[1,16,8192]{2,1,0:T(8,128)...) custom-call(s32[16]{0:T(128)} %owner_ref.1, s32[1,128]{1,0:T(1,128)} %bitcast.1, ...), custom_call_target="tpu_custom_call" | custom-call | tf_op jit(solution)/shard_map/pallas_call | solution.py:518
  101.5 2.9 %shard_map.163 = (bf16[128,1024]{1,0:T(8,128)(2,1)}, bf16[16,16,1024]{2,1,0:T(8,128)(2,1)}, bf16[16,16,1024]{2,1,0:T(8,128)(2,1)}, f32[1,16,8192]{2,1,0:T(8,128)...) custom-call(bf16[128,1024]{1,0:T(8,128)(2,1)} %get-tuple-element.14.refs_0_, ...), custom_call_target="tpu_custom_call" | custom-call | tf_op jit(solution)/shard_map/pallas_call | solution.py:582
where the time goes:
time: 106 us; the launch traced here: 104 us
  Pallas kernels  104 us (98%)
    pallas_call x1, Pallas kernels, on_device(): pl.pallas_call(functools.partial(kernel, n), out_shape=(shape((tokens, w)...  101 us
    pallas_call x1, Pallas kernels, on_device(): pl.pallas_call(hand_out, out_shape=tuple((shape(r.shape, r.dtype) for r i...  2.93 us

commit v1 on v0

--- a/solution.py
+++ b/solution.py
@@ -18,7 +18,8 @@
 correct_one = 1.0 - beta_one**20
 correct_two = 1.0 - beta_two**20
 
-CHUNKS = 2
+CHUNKS = 4
+EARLY = 2
 
 
 def adam_step(gradient, factor, moment, square):
@@ -31,35 +32,49 @@
     return (moment_next, square_next, change)
 
 
-def line_order(line):
+def block_order(line, zi):
+    low = zi < line // 2
+    near = jnp.where(low, zi, line - 1 - zi)
     order = []
-    for near in range((line + 1) // 2):
-        order.append(line - 1 - near)
-        if near != line - 1 - near:
-            order.append(near)
+    for k in range(line - 1):
+        far_first = line - 1 - (k // 2 if k % 2 == 0 else k // 2)
+        paired = far_first if k % 2 == 0 else k // 2
+        alone = line - 1 - (k - near)
+        place = jnp.where(k < 2 * near, paired, alone)
+        order.append(jnp.where(low, place, line - 1 - place))
+    order.append(zi)
     return order
 
 
 def kernel(
     n,
+    owner_hbm,
+    tenant_hbm,
+    feat_hbm,
+    cot_hbm,
+    down_hbm,
+    up_hbm,
+    weight_ref,
+    mom_down_ref,
+    mom_up_ref,
+    var_down_ref,
+    var_up_ref,
+    proj_hbm,
+    new_down_hbm,
+    new_up_hbm,
+    mean_down_ref,
+    mean_up_ref,
+    power_down_ref,
+    power_up_ref,
     owner_ref,
     tenant_ref,
     feat_ref,
     cot_ref,
     down_ref,
     up_ref,
-    weight_ref,
-    mom_down_ref,
-    mom_up_ref,
-    var_down_ref,
-    var_up_ref,
     proj_ref,
     new_down_ref,
     new_up_ref,
-    mean_down_ref,
-    mean_up_ref,
-    power_down_ref,
-    power_up_ref,
     wbuf,
     state,
     rpart,
@@ -76,6 +91,8 @@
     going_up,
     going_down,
     adapted,
+    isem,
+    osem,
     wsem,
     msem,
     rank_s,
@@ -97,20 +114,12 @@
     tenants, lowrank, w = down_ref.shape
     tokens, depth = feat_ref.shape
     line = n // 2
-    order = line_order(line)
     t = lax.axis_index("tensor")
     d = lax.axis_index("dp")
     zi, yi = t // 2, lax.rem(t, 2)
     mate = {"dp": 1 - d}
     pair = {"tensor": zi * 2 + 1 - yi}
-
-    quarter = max(1, line // 4)
-    waves = (
-        order[:quarter],
-        order[quarter : 2 * quarter],
-        order[2 * quarter : 3 * quarter],
-        order[3 * quarter :],
-    )
+    order = block_order(line, zi)
     height = tokens // CHUNKS
     paired = n & (n - 1) == 0
 
@@ -130,6 +139,22 @@
         pl.semaphore_signal(barrier, inc=1, device_id={"tensor": peer(o)}, device_id_type=MESH)
 
     pl.semaphore_signal(barrier, inc=1, device_id=mate, device_id_type=MESH)
+
+    in_copies = [
+        pltpu.make_async_copy(src, dst, isem.at[i])
+        for i, (src, dst) in enumerate(
+            (
+                (tenant_hbm, tenant_ref),
+                (feat_hbm, feat_ref),
+                (down_hbm, down_ref),
+                (cot_hbm, cot_ref),
+                (up_hbm, up_ref),
+                (owner_hbm, owner_ref),
+            )
+        )
+    ]
+    for copy in in_copies:
+        copy.start()
 
     def weight_copy(i, block):
         return pltpu.make_async_copy(
@@ -146,6 +171,7 @@
     for copy in state_copies:
         copy.start()
 
+    in_copies[0].wait()
     tenant = tenant_ref[...]
     contract = (((1,), (1,)), ((), ()))
     tenant_row = lax.broadcasted_iota(jnp.int32, (tenants, lowrank, tokens), 0)
@@ -160,8 +186,13 @@
         ).reshape(tenants, lowrank, tokens)
         return jnp.sum(jnp.where(tenant_hit, scores, 0.0), axis=0)
 
+    in_copies[1].wait()
+    in_copies[2].wait()
     rpart[0] = rank_part(down_ref, feat_ref)
+    in_copies[3].wait()
+    in_copies[4].wait()
     rpart[1] = rank_part(up_ref, cot_ref)
+    in_copies[5].wait()
 
     pl.semaphore_wait(barrier, n)
 
@@ -202,7 +233,7 @@
 
     for i, z in enumerate(order):
         ysend[z] = frozen(i, blocks[i])
-        if z in waves[0]:
+        if i == 0:
             pair_start(z)
 
     slot = jnp.zeros_like(tenant)
@@ -271,8 +302,7 @@
     def _(o):
         grad_copy(o, t).start()
 
-    for z in waves[1]:
-        pair_start(z)
+    pair_start(order[1])
 
     owned[t] = summed[t]
 
@@ -305,38 +335,40 @@
             device_id_type=MESH,
         )
 
-    def ends(z):
-        for c in range(CHUNKS):
-            at = rows_of(c)
-            pair_copy(z, c).wait_recv()
-            part[z, at] = part[z, at] + yrecv[z, at]
-
-            @pl.when(jnp.logical_and(zi == 0, z > 0))
-            def _():
-                up_copy(z, c).start()
-
-            @pl.when(jnp.logical_and(zi == line - 1, z < line - 1))
-            def _():
-                down_copy(z, c).start()
-
-    def middles(z):
-        for c in range(CHUNKS):
-            at = rows_of(c)
-
-            @pl.when(jnp.logical_and(zi > 0, zi < z))
-            def _():
-                up_copy(z, c).wait_recv()
-                part[z, at] = part[z, at] + going_up[z, at]
-                up_copy(z, c).start()
-
-            @pl.when(jnp.logical_and(zi > z, zi < line - 1))
-            def _():
-                down_copy(z, c).wait_recv()
-                part[z, at] = part[z, at] + going_down[z, at]
-                down_copy(z, c).start()
-
-    for z in waves[0]:
-        ends(z)
+    def pair_add(z, c):
+        at = rows_of(c)
+        pair_copy(z, c).wait_recv()
+        part[z, at] = part[z, at] + yrecv[z, at]
+
+    def ends(z, c):
+        @pl.when(jnp.logical_and(zi == 0, z > 0))
+        def _():
+            up_copy(z, c).start()
+
+        @pl.when(jnp.logical_and(zi == line - 1, z < line - 1))
+        def _():
+            down_copy(z, c).start()
+
+    def middles(z, c):
+        at = rows_of(c)
+
+        @pl.when(jnp.logical_and(zi > 0, zi < z))
+        def _():
+            up_copy(z, c).wait_recv()
+            part[z, at] = part[z, at] + going_up[z, at]
+            up_copy(z, c).start()
+
+        @pl.when(jnp.logical_and(zi > z, zi < line - 1))
+        def _():
+            down_copy(z, c).wait_recv()
+            part[z, at] = part[z, at] + going_down[z, at]
+            down_copy(z, c).start()
+
+    for c in range(CHUNKS):
+        pair_add(order[0], c)
+        ends(order[0], c)
+    for c in range(EARLY):
+        middles(order[0], c)
 
     for copy in state_copies:
         copy.wait()
@@ -344,9 +376,6 @@
     @pl.loop(1, n)
     def _(o):
         grad_copy(o, giver(o)).wait_recv()
-
-    for z in waves[2]:
-        pair_start(z)
 
     def squares_of(k, acc):
         g = owned[k]
@@ -388,6 +417,9 @@
     change_copy(n - 1, t).start()
     changes[t * 2 + d] = change[t]
 
+    for z in order[2:]:
+        pair_start(z)
+
     def forward_copy(source, side):
         at = source * 2 + side
         return pltpu.make_async_remote_copy(
@@ -407,24 +439,23 @@
     for copy in state_outs:
         copy.start()
 
-    for z in waves[3]:
-        pair_start(z)
-    for z in waves[1]:
-        ends(z)
-    for z in waves[0]:
-        middles(z)
-    for z in waves[2]:
-        ends(z)
+    for c in range(EARLY, CHUNKS):
+        middles(order[0], c)
+    for c in range(CHUNKS):
+        pair_add(order[1], c)
+        ends(order[1], c)
+        middles(order[1], c)
 
     @pl.loop(1, n)
     def _(o):
         change_copy(o, giver(o)).wait_recv()
         forward_copy(giver(o), d).start()
 
-    for z in waves[3]:
-        ends(z)
-    for z in waves[1] + waves[2]:
-        middles(z)
+    for z in order[2:-1]:
+        for c in range(CHUNKS):
+            pair_add(z, c)
+            ends(z, c)
+            middles(z, c)
 
     @pl.loop(0, n)
     def _(source):
@@ -436,11 +467,20 @@
         new_down_ref[k] = (down_ref[k].astype(jnp.float32) - back[0]).astype(jnp.bfloat16)
         new_up_ref[k] = (up_ref[k].astype(jnp.float32) - back[1]).astype(jnp.bfloat16)
 
-    for z in waves[3]:
-        middles(z)
+    adapter_outs = [
+        pltpu.make_async_copy(new_down_ref, new_down_hbm, osem.at[0]),
+        pltpu.make_async_copy(new_up_ref, new_up_hbm, osem.at[1]),
+    ]
+    for copy in adapter_outs:
+        copy.start()
+
+    def proj_out(c):
+        at = rows_of(c)
+        return pltpu.make_async_copy(proj_ref.at[at], proj_hbm.at[at], osem.at[2 + c])
 
     for c in range(CHUNKS):
         at = rows_of(c)
+        pair_add(zi, c)
 
         @pl.when(zi > 0)
         def _():
@@ -453,8 +493,9 @@
             part[zi, at] = part[zi, at] + going_down[zi, at]
 
         proj_ref[at] = (part[zi, at] + adapted[at]).astype(proj_ref.dtype)
-
-    for copy in state_outs:
+        proj_out(c).start()
+
+    for copy in state_outs + adapter_outs:
         copy.wait()
 
     @pl.loop(1, n)
@@ -469,13 +510,16 @@
 
     for i in range(2):
         mate_copy(i).wait_send()
-    for z in order:
+    for z in range(line):
         for c in range(CHUNKS):
             pair_copy(z, c).wait_send()
 
             @pl.when(zi != z)
             def _():
                 up_copy(z, c).wait_send()
+
+    for c in range(CHUNKS):
+        proj_out(c).wait()
 
 
 def hand_out(*refs):
@@ -511,7 +555,7 @@
     tenants, lowrank, w = adapter_down.shape
     line = n // 2
     f32 = jnp.float32
-    vmem = pl.BlockSpec(memory_space=pltpu.VMEM)
+    bf16 = jnp.bfloat16
     hbm = pl.BlockSpec(memory_space=pl.ANY)
     dma = pltpu.SemaphoreType.DMA
     shape = jax.ShapeDtypeStruct
@@ -526,9 +570,18 @@
             shape(variance_down.shape, f32),
             shape(variance_up.shape, f32),
         ),
-        in_specs=[pl.BlockSpec(memory_space=pltpu.SMEM)] + [vmem] * 5 + [hbm] * 5,
-        out_specs=[vmem] * 3 + [hbm] * 4,
+        in_specs=[hbm] * 11,
+        out_specs=[hbm] * 7,
         scratch_shapes=[
+            pltpu.SMEM((tenants,), jnp.int32),
+            pltpu.VMEM((1, tokens), jnp.int32),
+            pltpu.VMEM((tokens, depth), bf16),
+            pltpu.VMEM((tokens, w), bf16),
+            pltpu.VMEM(adapter_down.shape, bf16),
+            pltpu.VMEM(adapter_up.shape, bf16),
+            pltpu.VMEM((tokens, w), bf16),
+            pltpu.VMEM(adapter_down.shape, bf16),
+            pltpu.VMEM(adapter_up.shape, bf16),
             pltpu.VMEM((n, depth, w), jnp.bfloat16),
             pltpu.VMEM((4,) + momentum_down.shape, f32),
             pltpu.VMEM((2, lowrank, tokens), f32),
@@ -545,6 +598,8 @@
             pltpu.VMEM((line, tokens, w), f32),
             pltpu.VMEM((line, tokens, w), f32),
             pltpu.VMEM((tokens, w), f32),
+            dma((6,)),
+            dma((2 + CHUNKS,)),
             dma((n,)),
             dma((4,)),
             dma((n,)),

time: 106 us -> 91.1 us (0.86); the launches traced: 104 us -> 91 us
  Pallas kernels: 104 us -> 90.3 us
    pallas_call x1, Pallas kernels: 101 us -> 87.4 us  [on_device(): pl.pallas_call(functools.partial(kernel, n), out_shape=(shape((tokens, w)...]
where the time goes in v1:
time: 91.1 us; the launch traced here: 91 us
  Pallas kernels  90.3 us (99%)
    pallas_call x1, Pallas kernels, on_device(): pl.pallas_call(functools.partial(kernel, n), out_shape=(shape((tokens, w)...  87.4 us
    pallas_call x1, Pallas kernels, on_device(): pl.pallas_call(hand_out, out_shape=tuple((shape(r.shape, r.dtype) for r i...  2.93 us

profile of v1, /device:TPU:9, one launch (start us, length us, event | category | flops | bytes accessed | tf_op | source)
XLA Modules:
  0.0 91.0 jit_solution(1265150050511635253)
XLA Ops:
  0.6 87.4 %shard_map.162 = (bf16[128,1024]{1,0:T(8,128)(2,1)}, bf16[16,16,1024]{2,1,0:T(8,128)(2,1)}, bf16[16,16,1024]{2,1,0:T(8,128)(2,1)}, f32[1,16,8192]{2,1,0:T(8,128)...) custom-call(s32[16]{0:T(128)} %owner_hbm.1, s32[1,128]{1,0:T(1,128)} %bitcast.1, ...), custom_call_target="tpu_custom_call" | custom-call | tf_op jit(solution)/shard_map/pallas_call | solution.py:562
  88.0 2.9 %shard_map.163 = (bf16[128,1024]{1,0:T(8,128)(2,1)}, bf16[16,16,1024]{2,1,0:T(8,128)(2,1)}, bf16[16,16,1024]{2,1,0:T(8,128)(2,1)}, f32[1,16,8192]{2,1,0:T(8,128)...) custom-call(bf16[128,1024]{1,0:T(8,128)(2,1)} %get-tuple-element.14.refs_0_, ...), custom_call_target="tpu_custom_call" | custom-call | tf_op jit(solution)/shard_map/pallas_call | solution.py:637

commit v2 on v1

--- a/solution.py
+++ b/solution.py
@@ -19,7 +19,8 @@
 correct_two = 1.0 - beta_two**20
 
 CHUNKS = 4
-EARLY = 2
+EARLY = 1
+INNER = ((1, 0), (1, 1), (2, 0), (2, 1), (1, 2), (2, 2), (1, 3), (2, 3))
 
 
 def adam_step(gradient, factor, moment, square):
@@ -162,6 +163,26 @@
         )
 
     blocks = [z * 2 + 1 - yi for z in order] + [z * 2 + yi for z in order]
+    in_copies[0].wait()
+    tenant = tenant_ref[...]
+    contract = (((1,), (1,)), ((), ()))
+    tenant_row = lax.broadcasted_iota(jnp.int32, (tenants, lowrank, tokens), 0)
+    tenant_hit = tenant_row == tenant[None]
+
+    def rank_part(adapter, rows):
+        scores = lax.dot_general(
+            adapter[...].reshape(tenants * lowrank, w),
+            rows[...],
+            contract,
+            preferred_element_type=jnp.float32,
+        ).reshape(tenants, lowrank, tokens)
+        return jnp.sum(jnp.where(tenant_hit, scores, 0.0), axis=0)
+
+    in_copies[1].wait()
+    in_copies[2].wait()
+    rpart[0] = rank_part(down_ref, feat_ref)
+    in_copies[3].wait()
+    in_copies[4].wait()
     for i, block in enumerate(blocks):
         weight_copy(i, block).start()
     state_copies = [
@@ -170,27 +191,6 @@
     ]
     for copy in state_copies:
         copy.start()
-
-    in_copies[0].wait()
-    tenant = tenant_ref[...]
-    contract = (((1,), (1,)), ((), ()))
-    tenant_row = lax.broadcasted_iota(jnp.int32, (tenants, lowrank, tokens), 0)
-    tenant_hit = tenant_row == tenant[None]
-
-    def rank_part(adapter, rows):
-        scores = lax.dot_general(
-            adapter[...].reshape(tenants * lowrank, w),
-            rows[...],
-            contract,
-            preferred_element_type=jnp.float32,
-        ).reshape(tenants, lowrank, tokens)
-        return jnp.sum(jnp.where(tenant_hit, scores, 0.0), axis=0)
-
-    in_copies[1].wait()
-    in_copies[2].wait()
-    rpart[0] = rank_part(down_ref, feat_ref)
-    in_copies[3].wait()
-    in_copies[4].wait()
     rpart[1] = rank_part(up_ref, cot_ref)
     in_copies[5].wait()
 
@@ -200,7 +200,7 @@
         return pltpu.make_async_remote_copy(
             src_ref=rpart,
             dst_ref=rbuf.at[source],
-            send_sem=rank_s.at[o],
+            send_sem=rank_s.at[0],
             recv_sem=rank_r.at[source],
             device_id={"tensor": peer(o)},
             device_id_type=MESH,
@@ -217,7 +217,7 @@
         return pltpu.make_async_remote_copy(
             src_ref=ysend.at[z, rows_of(c)],
             dst_ref=yrecv.at[z, rows_of(c)],
-            send_sem=y_s.at[z * CHUNKS + c],
+            send_sem=y_s.at[0],
             recv_sem=y_r.at[z * CHUNKS + c],
             device_id=pair,
             device_id_type=MESH,
@@ -255,52 +255,46 @@
 
     half_row = lax.broadcasted_iota(jnp.int32, (n, lowrank, tokens), 0) * 2
 
-    def half_grads(side):
+    def half_grads(side, values, rows):
         hit = half_row + side == slot[None]
-
-        def one(values, rows):
-            spread = jnp.where(hit, values[None], 0.0).reshape(n * lowrank, tokens)
-            return jnp.dot(
-                spread.astype(jnp.bfloat16), rows[...], preferred_element_type=jnp.float32
-            ).reshape(n, lowrank, w)
-
-        return one(up_low, feat_ref), one(down_low, cot_ref)
+        spread = jnp.where(hit, values[None], 0.0).reshape(n * lowrank, tokens)
+        return jnp.dot(
+            spread.astype(jnp.bfloat16), rows[...], preferred_element_type=jnp.float32
+        ).reshape(n, lowrank, w)
 
     def mate_copy(i):
         return pltpu.make_async_remote_copy(
             src_ref=gsend.at[i],
             dst_ref=grecv.at[i],
-            send_sem=g_s.at[i],
+            send_sem=g_s.at[0],
             recv_sem=g_r.at[i],
             device_id=mate,
             device_id_type=MESH,
         )
 
-    theirs = half_grads(1 - d)
+    def grad_copy(o, source, side):
+        return pltpu.make_async_remote_copy(
+            src_ref=summed.at[peer(o), side],
+            dst_ref=owned.at[source, side],
+            send_sem=a_s.at[0],
+            recv_sem=a_r.at[source],
+            device_id={"tensor": peer(o)},
+            device_id_type=MESH,
+        )
+
+    both = pl.ds(0, 2)
+    sides = ((up_low, feat_ref), (down_low, cot_ref))
     for i in range(2):
-        gsend[i] = theirs[i]
+        gsend[i] = half_grads(1 - d, *sides[i])
+        mate_copy(i).start()
     for i in range(2):
-        mate_copy(i).start()
-    mine = half_grads(d)
-    for i in range(2):
-        summed[:, i] = mine[i]
-    for i in range(2):
+        summed[:, i] = half_grads(d, *sides[i])
         mate_copy(i).wait_recv()
         summed[:, i] = summed[:, i] + grecv[i]
 
-    def grad_copy(o, source):
-        return pltpu.make_async_remote_copy(
-            src_ref=summed.at[peer(o)],
-            dst_ref=owned.at[source],
-            send_sem=a_s.at[o],
-            recv_sem=a_r.at[source],
-            device_id={"tensor": peer(o)},
-            device_id_type=MESH,
-        )
-
-    @pl.loop(1, n)
-    def _(o):
-        grad_copy(o, t).start()
+        @pl.loop(1, n)
+        def _(o):
+            grad_copy(o, t, i).start()
 
     pair_start(order[1])
 
@@ -319,7 +313,7 @@
         return pltpu.make_async_remote_copy(
             src_ref=part.at[z, rows_of(c)],
             dst_ref=going_up.at[z, rows_of(c)],
-            send_sem=z_s.at[z * CHUNKS + c],
+            send_sem=z_s.at[0],
             recv_sem=u_r.at[z * CHUNKS + c],
             device_id={"tensor": lax.rem(t + 2, n)},
             device_id_type=MESH,
@@ -329,7 +323,7 @@
         return pltpu.make_async_remote_copy(
             src_ref=part.at[z, rows_of(c)],
             dst_ref=going_down.at[z, rows_of(c)],
-            send_sem=z_s.at[z * CHUNKS + c],
+            send_sem=z_s.at[0],
             recv_sem=d_r.at[z * CHUNKS + c],
             device_id={"tensor": lax.rem(t + n - 2, n)},
             device_id_type=MESH,
@@ -375,7 +369,7 @@
 
     @pl.loop(1, n)
     def _(o):
-        grad_copy(o, giver(o)).wait_recv()
+        grad_copy(o, giver(o), both).wait_recv()
 
     def squares_of(k, acc):
         g = owned[k]
@@ -389,7 +383,7 @@
         return pltpu.make_async_remote_copy(
             src_ref=change.at[peer(o)],
             dst_ref=changes.at[source * 2 + d],
-            send_sem=c_s.at[o],
+            send_sem=c_s.at[0],
             recv_sem=c_r.at[source],
             device_id={"tensor": peer(o)},
             device_id_type=MESH,
@@ -425,7 +419,7 @@
         return pltpu.make_async_remote_copy(
             src_ref=changes.at[at],
             dst_ref=changes.at[at],
-            send_sem=f_s.at[source],
+            send_sem=f_s.at[0],
             recv_sem=f_r.at[source],
             device_id=mate,
             device_id_type=MESH,
@@ -439,23 +433,33 @@
     for copy in state_outs:
         copy.start()
 
-    for c in range(EARLY, CHUNKS):
-        middles(order[0], c)
-    for c in range(CHUNKS):
-        pair_add(order[1], c)
-        ends(order[1], c)
-        middles(order[1], c)
+    inner = jnp.logical_and(zi > 0, zi < line - 1)
+
+    @pl.when(inner)
+    def _():
+        for c in range(EARLY, CHUNKS):
+            middles(order[0], c)
+        for k, c in INNER:
+            pair_add(order[k], c)
+            middles(order[k], c)
+
+    @pl.when(jnp.logical_not(inner))
+    def _():
+        for k in (1, 2):
+            for c in range(CHUNKS):
+                pair_add(order[k], c)
+                ends(order[k], c)
+
+    for z in order[3:-1]:
+        for c in range(CHUNKS):
+            pair_add(z, c)
+            ends(z, c)
+            middles(z, c)
 
     @pl.loop(1, n)
     def _(o):
         change_copy(o, giver(o)).wait_recv()
         forward_copy(giver(o), d).start()
-
-    for z in order[2:-1]:
-        for c in range(CHUNKS):
-            pair_add(z, c)
-            ends(z, c)
-            middles(z, c)
 
     @pl.loop(0, n)
     def _(source):
@@ -498,41 +502,26 @@
     for copy in state_outs + adapter_outs:
         copy.wait()
 
-    @pl.loop(1, n)
-    def _(o):
-        rank_copy(o, t).wait_send()
-        grad_copy(o, t).wait_send()
-        change_copy(o, t).wait_send()
-
-    @pl.loop(0, n)
-    def _(source):
-        forward_copy(source, d).wait_send()
-
-    for i in range(2):
-        mate_copy(i).wait_send()
-    for z in range(line):
-        for c in range(CHUNKS):
-            pair_copy(z, c).wait_send()
-
-            @pl.when(zi != z)
-            def _():
-                up_copy(z, c).wait_send()
-
+    def sent(ref, sem):
+        pltpu.make_async_copy(ref, ref, sem).wait()
+
+    sent(rbuf.at[pl.ds(0, n - 1)], rank_s.at[0])
+    sent(gsend, g_s.at[0])
+    sent(change.at[pl.ds(0, n - 1)], a_s.at[0])
+    sent(change.at[pl.ds(0, n - 1)], c_s.at[0])
+    sent(changes.at[pl.ds(0, n)], f_s.at[0])
+    sent(ysend, y_s.at[0])
+    sent(part.at[pl.ds(0, line - 1)], z_s.at[0])
     for c in range(CHUNKS):
         proj_out(c).wait()
 
 
 def hand_out(*refs):
-    count = len(refs) // 3
-    sources, results, held = refs[:count], refs[count : 2 * count], refs[2 * count : 3 * count]
+    count = len(refs) // 2
     sems = refs[-1]
-    ins = [pltpu.make_async_copy(sources[i], held[i], sems.at[0, i]) for i in range(count)]
-    outs = [pltpu.make_async_copy(held[i], results[i], sems.at[1, i]) for i in range(count)]
-    for copy in ins:
+    outs = [pltpu.make_async_copy(refs[i], refs[count + i], sems.at[i]) for i in range(count)]
+    for copy in outs:
         copy.start()
-    for i in range(count):
-        ins[i].wait()
-        outs[i].start()
     for copy in outs:
         copy.wait()
 
@@ -556,7 +545,8 @@
     line = n // 2
     f32 = jnp.float32
     bf16 = jnp.bfloat16
-    hbm = pl.BlockSpec(memory_space=pl.ANY)
+    hbm = pl.BlockSpec(memory_space=pltpu.HBM)
+    anywhere = pl.BlockSpec(memory_space=pl.ANY)
     dma = pltpu.SemaphoreType.DMA
     shape = jax.ShapeDtypeStruct
     results = pl.pallas_call(
@@ -571,7 +561,7 @@
             shape(variance_up.shape, f32),
         ),
         in_specs=[hbm] * 11,
-        out_specs=[hbm] * 7,
+        out_specs=[anywhere] * 7,
         scratch_shapes=[
             pltpu.SMEM((tenants,), jnp.int32),
             pltpu.VMEM((1, tokens), jnp.int32),
@@ -602,45 +592,50 @@
             dma((2 + CHUNKS,)),
             dma((n,)),
             dma((4,)),
+            dma((1,)),
             dma((n,)),
+            dma((1,)),
+            dma((2,)),
+            dma((1,)),
             dma((n,)),
-            dma((2,)),
-            dma((2,)),
+            dma((1,)),
             dma((n,)),
+            dma((1,)),
             dma((n,)),
-            dma((n,)),
-            dma((n,)),
-            dma((n,)),
-            dma((n,)),
+            dma((1,)),
             dma((line * CHUNKS,)),
-            dma((line * CHUNKS,)),
-            dma((line * CHUNKS,)),
+            dma((1,)),
             dma((line * CHUNKS,)),
             dma((line * CHUNKS,)),
         ],
         compiler_params=pltpu.CompilerParams(
-            collective_id=0, has_side_effects=True, vmem_limit_bytes=60 * 1024 * 1024
+            collective_id=0, has_side_effects=True, vmem_limit_bytes=48 * 1024 * 1024
         ),
     )(
-        owner_device,
-        token_tenant.reshape(1, tokens),
-        features,
-        cotangent,
-        adapter_down,
-        adapter_up,
-        frozen_weight,
-        momentum_down,
-        momentum_up,
-        variance_down,
-        variance_up,
+        *(
+            pltpu.with_memory_space_constraint(x, pltpu.HBM)
+            for x in (
+                owner_device,
+                token_tenant.reshape(1, tokens),
+                features,
+                cotangent,
+                adapter_down,
+                adapter_up,
+                frozen_weight,
+                momentum_down,
+                momentum_up,
+                variance_down,
+                variance_up,
+            )
+        )
     )
     return pl.pallas_call(
         hand_out,
         out_shape=tuple(shape(r.shape, r.dtype) for r in results),
-        in_specs=[hbm] * len(results),
+        in_specs=[anywhere] * len(results),
         out_specs=[hbm] * len(results),
-        scratch_shapes=[pltpu.VMEM(r.shape, r.dtype) for r in results]
-        + [dma((2, len(results)))],
+        scratch_shapes=[dma((len(results),))],
+        compiler_params=pltpu.CompilerParams(vmem_limit_bytes=1024 * 1024),
     )(*results)
 
 

time: 91.1 us -> 83.4 us (0.915)
  Pallas kernels: 90.3 us -> 82.5 us
    pallas_call x1, Pallas kernels: 87.4 us -> 80.7 us  [on_device(): pl.pallas_call(functools.partial(kernel, n), out_shape=(shape((tokens, w)...]
    pallas_call x1, Pallas kernels: 2.93 us -> 1.81 us  [on_device(): pl.pallas_call(hand_out, out_shape=tuple((shape(r.shape, r.dtype) for r i...]
where the time goes in v2:
time: 83.4 us; the launch traced here: 83.2 us
  Pallas kernels  82.5 us (99%)
    pallas_call x1, Pallas kernels, on_device(): pl.pallas_call(functools.partial(kernel, n), out_shape=(shape((tokens, w)...  80.7 us
    pallas_call x1, Pallas kernels, on_device(): pl.pallas_call(hand_out, out_shape=tuple((shape(r.shape, r.dtype) for r i...  1.81 us

profile of v2, /device:TPU:9, one launch (start us, length us, event | category | flops | bytes accessed | tf_op | source)
XLA Modules:
  0.0 83.2 jit_solution(12586133537823242492)
XLA Ops:
  0.6 80.7 %shard_map.162 = (bf16[128,1024]{1,0:T(8,128)(2,1)S(1)}, bf16[16,16,1024]{2,1,0:T(8,128)(2,1)S(1)}, bf16[16,16,1024]{2,1,0:T(8,128)(2,1)S(1)}, f32[1,16,8192]{2,...) custom-call(s32[16]{0:T(128)} %owner_hbm.1, ...), custom_call_target="tpu_custom_call" | custom-call | tf_op jit(solution)/shard_map/pallas_call | solution.py:552
  81.4 1.8 %shard_map.163 = (bf16[128,1024]{1,0:T(8,128)(2,1)}, bf16[16,16,1024]{2,1,0:T(8,128)(2,1)}, bf16[16,16,1024]{2,1,0:T(8,128)(2,1)}, f32[1,16,8192]{2,1,0:T(8,128)...) custom-call(bf16[128,1024]{1,0:T(8,128)(2,1)S(1)} %get-tuple-element.14.refs_0_, ...), custom_call_target="tpu_custom_call" | custom-call | tf_op jit(solution)/shard_map/pallas_call | solution.py:632

commit v3 on v2

--- a/solution.py
+++ b/solution.py
@@ -20,6 +20,7 @@
 
 CHUNKS = 4
 EARLY = 1
+LEND_AT = 3
 INNER = ((1, 0), (1, 1), (2, 0), (2, 1), (1, 2), (2, 2), (1, 3), (2, 3))
 
 
@@ -69,8 +70,8 @@
     power_up_ref,
     owner_ref,
     tenant_ref,
-    feat_ref,
-    cot_ref,
+    mate_tenant,
+    rows_ref,
     down_ref,
     up_ref,
     proj_ref,
@@ -80,8 +81,10 @@
     state,
     rpart,
     rbuf,
-    gsend,
-    grecv,
+    raw_out,
+    raw_in,
+    low_out,
+    low_in,
     summed,
     owned,
     change,
@@ -92,6 +95,9 @@
     going_up,
     going_down,
     adapted,
+    lent,
+    scale_out,
+    scale_in,
     isem,
     osem,
     wsem,
@@ -109,11 +115,15 @@
     y_s,
     y_r,
     z_s,
-    u_r,
-    d_r,
+    z_r,
+    l_s,
+    l_r,
+    h_s,
+    s_r,
 ):
     tenants, lowrank, w = down_ref.shape
-    tokens, depth = feat_ref.shape
+    tokens = tenant_ref.shape[1]
+    feat_ref, cot_ref = (rows_ref.at[i, pl.ds(0, tokens)] for i in range(2))
     line = n // 2
     t = lax.axis_index("tensor")
     d = lax.axis_index("dp")
@@ -122,6 +132,11 @@
     pair = {"tensor": zi * 2 + 1 - yi}
     order = block_order(line, zi)
     height = tokens // CHUNKS
+    low_side = zi < line // 2
+    lent_to = jnp.where(low_side, t + 2, t - 2)
+    lent_way = jnp.where(low_side, 0, 1)
+    from_below = jnp.logical_and(zi > 0, zi - 1 < line // 2)
+    from_above = jnp.logical_and(zi < line - 1, zi + 1 >= line // 2)
     paired = n & (n - 1) == 0
 
     def peer(o):
@@ -133,13 +148,10 @@
     def columns(block):
         return pl.ds(pl.multiple_of(block * w, w), w)
 
+    def sent(ref, sem):
+        pltpu.make_async_copy(ref, ref, sem).wait()
+
     barrier = pltpu.get_barrier_semaphore()
-
-    @pl.loop(1, n)
-    def _(o):
-        pl.semaphore_signal(barrier, inc=1, device_id={"tensor": peer(o)}, device_id_type=MESH)
-
-    pl.semaphore_signal(barrier, inc=1, device_id=mate, device_id_type=MESH)
 
     in_copies = [
         pltpu.make_async_copy(src, dst, isem.at[i])
@@ -157,6 +169,12 @@
     for copy in in_copies:
         copy.start()
 
+    @pl.loop(1, n)
+    def _(o):
+        pl.semaphore_signal(barrier, inc=1, device_id={"tensor": peer(o)}, device_id_type=MESH)
+
+    pl.semaphore_signal(barrier, inc=1, device_id=mate, device_id_type=MESH)
+
     def weight_copy(i, block):
         return pltpu.make_async_copy(
             weight_ref.at[:, columns(block)], wbuf.at[i], wsem.at[i]
@@ -178,20 +196,20 @@
         ).reshape(tenants, lowrank, tokens)
         return jnp.sum(jnp.where(tenant_hit, scores, 0.0), axis=0)
 
-    in_copies[1].wait()
-    in_copies[2].wait()
-    rpart[0] = rank_part(down_ref, feat_ref)
-    in_copies[3].wait()
-    in_copies[4].wait()
+    for copy in in_copies[1:5]:
+        copy.wait()
     for i, block in enumerate(blocks):
         weight_copy(i, block).start()
     state_copies = [
-        pltpu.make_async_copy(ref, state.at[i], msem.at[i])
+        pltpu.make_async_copy(ref, state.at[i], msem.at[0])
         for i, ref in enumerate((mom_down_ref, mom_up_ref, var_down_ref, var_up_ref))
     ]
     for copy in state_copies:
         copy.start()
-    rpart[1] = rank_part(up_ref, cot_ref)
+    down_part = rank_part(down_ref, feat_ref)
+    up_part = rank_part(up_ref, cot_ref)
+    rpart[0] = down_part
+    rpart[1] = up_part
     in_copies[5].wait()
 
     pl.semaphore_wait(barrier, n)
@@ -210,6 +228,34 @@
     def _(o):
         rank_copy(o, t).start()
 
+    def mate_copy(source, target, out, arrived):
+        return pltpu.make_async_remote_copy(
+            src_ref=source,
+            dst_ref=target,
+            send_sem=g_s.at[out],
+            recv_sem=g_r.at[arrived],
+            device_id=mate,
+            device_id_type=MESH,
+        )
+
+    tenant_copy = mate_copy(tenant_ref, mate_tenant, 0, 0)
+    raw_copies = [mate_copy(raw_out.at[i], raw_in.at[i], 1, 1 + i) for i in range(2)]
+    low_copy = mate_copy(low_out, low_in, 2, 3)
+    tenant_copy.start()
+    for i, rows in enumerate((feat_ref, cot_ref)):
+        raw_out[i] = rows[...].astype(jnp.float32)
+        raw_copies[i].start()
+
+    def lent_copy(i):
+        return pltpu.make_async_remote_copy(
+            src_ref=(mom_down_ref, var_down_ref)[i].at[0, :, columns(lent_to)],
+            dst_ref=lent.at[lent_way, i],
+            send_sem=l_s.at[0],
+            recv_sem=l_r.at[lent_way],
+            device_id={"tensor": lent_to},
+            device_id_type=MESH,
+        )
+
     def rows_of(c):
         return pl.ds(c * height, height)
 
@@ -235,11 +281,23 @@
         ysend[z] = frozen(i, blocks[i])
         if i == 0:
             pair_start(z)
-
-    slot = jnp.zeros_like(tenant)
-    slot = lax.fori_loop(
-        0, tenants, lambda k, s: jnp.where(tenant == k, owner_ref[k], s), slot
+        if i == LEND_AT:
+            for k in range(2):
+                lent_copy(k).start()
+
+    tenant_copy.wait_recv()
+    tenants_here = (tenant, mate_tenant[...])
+    slots = lax.fori_loop(
+        0,
+        tenants,
+        lambda k, found: tuple(
+            jnp.where(here == k, owner_ref[k], s) for here, s in zip(tenants_here, found)
+        ),
+        tuple(jnp.zeros_like(here) for here in tenants_here),
     )
+    for i in range(2):
+        raw_copies[i].wait_recv()
+        rows_ref[i, tokens:] = raw_in[i].astype(jnp.bfloat16)
 
     @pl.loop(1, n)
     def _(o):
@@ -253,24 +311,15 @@
     down_low = low[0].astype(jnp.bfloat16).astype(jnp.float32)
     up_low = low[1].astype(jnp.bfloat16).astype(jnp.float32)
 
-    half_row = lax.broadcasted_iota(jnp.int32, (n, lowrank, tokens), 0) * 2
-
-    def half_grads(side, values, rows):
-        hit = half_row + side == slot[None]
-        spread = jnp.where(hit, values[None], 0.0).reshape(n * lowrank, tokens)
-        return jnp.dot(
-            spread.astype(jnp.bfloat16), rows[...], preferred_element_type=jnp.float32
-        ).reshape(n, lowrank, w)
-
-    def mate_copy(i):
-        return pltpu.make_async_remote_copy(
-            src_ref=gsend.at[i],
-            dst_ref=grecv.at[i],
-            send_sem=g_s.at[0],
-            recv_sem=g_r.at[i],
-            device_id=mate,
-            device_id_type=MESH,
-        )
+    low_out[0] = up_low
+    low_out[1] = down_low
+    low_copy.start()
+
+    half_row = lax.broadcasted_iota(jnp.int32, (n, lowrank, tokens), 0) * 2 + d
+
+    def spread(values, slot):
+        picked = jnp.where(half_row == slot[None], values[None], 0.0)
+        return picked.reshape(n * lowrank, tokens).astype(jnp.bfloat16)
 
     def grad_copy(o, source, side):
         return pltpu.make_async_remote_copy(
@@ -283,14 +332,14 @@
         )
 
     both = pl.ds(0, 2)
-    sides = ((up_low, feat_ref), (down_low, cot_ref))
+    own_part = [spread(low, slots[0]) for low in (up_low, down_low)]
+    low_copy.wait_recv()
     for i in range(2):
-        gsend[i] = half_grads(1 - d, *sides[i])
-        mate_copy(i).start()
-    for i in range(2):
-        summed[:, i] = half_grads(d, *sides[i])
-        mate_copy(i).wait_recv()
-        summed[:, i] = summed[:, i] + grecv[i]
+        summed[:, i] = jnp.dot(
+            jnp.concatenate([own_part[i], spread(low_in[i], slots[1])], axis=1),
+            rows_ref[i],
+            preferred_element_type=jnp.float32,
+        ).reshape(n, lowrank, w)
 
         @pl.loop(1, n)
         def _(o):
@@ -314,20 +363,30 @@
             src_ref=part.at[z, rows_of(c)],
             dst_ref=going_up.at[z, rows_of(c)],
             send_sem=z_s.at[0],
-            recv_sem=u_r.at[z * CHUNKS + c],
+            recv_sem=z_r.at[z * CHUNKS + c],
             device_id={"tensor": lax.rem(t + 2, n)},
             device_id_type=MESH,
         )
 
-    def down_copy(z, c):
+    def down_copy(z, c, last=False):
+        slot_at = line if last else z
         return pltpu.make_async_remote_copy(
             src_ref=part.at[z, rows_of(c)],
             dst_ref=going_down.at[z, rows_of(c)],
             send_sem=z_s.at[0],
-            recv_sem=d_r.at[z * CHUNKS + c],
+            recv_sem=z_r.at[slot_at * CHUNKS + c],
             device_id={"tensor": lax.rem(t + n - 2, n)},
             device_id_type=MESH,
         )
+
+    def send_down(z, c):
+        @pl.when(z == zi - 1)
+        def _():
+            down_copy(z, c, True).start()
+
+        @pl.when(z < zi - 1)
+        def _():
+            down_copy(z, c).start()
 
     def pair_add(z, c):
         at = rows_of(c)
@@ -341,7 +400,7 @@
 
         @pl.when(jnp.logical_and(zi == line - 1, z < line - 1))
         def _():
-            down_copy(z, c).start()
+            send_down(z, c)
 
     def middles(z, c):
         at = rows_of(c)
@@ -356,7 +415,7 @@
         def _():
             down_copy(z, c).wait_recv()
             part[z, at] = part[z, at] + going_down[z, at]
-            down_copy(z, c).start()
+            send_down(z, c)
 
     for c in range(CHUNKS):
         pair_add(order[0], c)
@@ -364,8 +423,7 @@
     for c in range(EARLY):
         middles(order[0], c)
 
-    for copy in state_copies:
-        copy.wait()
+    sent(state, msem.at[0])
 
     @pl.loop(1, n)
     def _(o):
@@ -388,6 +446,36 @@
             device_id={"tensor": peer(o)},
             device_id_type=MESH,
         )
+
+    def half_copy(source):
+        return pltpu.make_async_remote_copy(
+            src_ref=change.at[lent_to, 1],
+            dst_ref=changes.at[source * 2 + d, 1],
+            send_sem=h_s.at[0],
+            recv_sem=c_r.at[source],
+            device_id={"tensor": lent_to},
+            device_id_type=MESH,
+        )
+
+    scale_copy = pltpu.make_async_remote_copy(
+        src_ref=scale_out,
+        dst_ref=scale_in.at[lent_way],
+        send_sem=h_s.at[1],
+        recv_sem=s_r.at[lent_way],
+        device_id={"tensor": lent_to},
+        device_id_type=MESH,
+    )
+    scale_out[...] = jnp.broadcast_to(factor, scale_out.shape)
+    scale_copy.start()
+
+    def change_start(o):
+        @pl.when(peer(o) != lent_to)
+        def _():
+            change_copy(o, t).start()
+
+        @pl.when(peer(o) == lent_to)
+        def _():
+            half_copy(t).start()
 
     def step_piece(k):
         at = columns(k)
@@ -405,10 +493,10 @@
 
         @pl.when(o > 1)
         def _():
-            change_copy(o - 1, t).start()
+            change_start(o - 1)
 
     step_piece(t)
-    change_copy(n - 1, t).start()
+    change_start(n - 1)
     changes[t * 2 + d] = change[t]
 
     for z in order[2:]:
@@ -427,7 +515,7 @@
 
     forward_copy(t, d).start()
     state_outs = [
-        pltpu.make_async_copy(state.at[i], ref, msem.at[i])
+        pltpu.make_async_copy(state.at[i], ref, msem.at[0])
         for i, ref in enumerate((mean_down_ref, mean_up_ref, power_down_ref, power_up_ref))
     ]
     for copy in state_outs:
@@ -458,8 +546,27 @@
 
     @pl.loop(1, n)
     def _(o):
-        change_copy(o, giver(o)).wait_recv()
-        forward_copy(giver(o), d).start()
+        source = giver(o)
+        below = jnp.logical_and(from_below, source == t - 2)
+        above = jnp.logical_and(from_above, source == t + 2)
+        borrowed = jnp.logical_or(below, above)
+
+        @pl.when(jnp.logical_not(borrowed))
+        def _():
+            change_copy(o, source).wait_recv()
+
+        @pl.when(borrowed)
+        def _():
+            way = jnp.where(below, 0, 1)
+            half_copy(source).wait_recv()
+            sent(scale_in.at[way], s_r.at[way])
+            sent(lent.at[way], l_r.at[way])
+            scale = scale_in[way]
+            changes[source * 2 + d, 0] = adam_step(
+                summed[source, 0], scale[:1, :1], lent[way, 0], lent[way, 1]
+            )[2]
+
+        forward_copy(source, d).start()
 
     @pl.loop(0, n)
     def _(source):
@@ -480,7 +587,7 @@
 
     def proj_out(c):
         at = rows_of(c)
-        return pltpu.make_async_copy(proj_ref.at[at], proj_hbm.at[at], osem.at[2 + c])
+        return pltpu.make_async_copy(proj_ref.at[at], proj_hbm.at[at], osem.at[2])
 
     for c in range(CHUNKS):
         at = rows_of(c)
@@ -493,27 +600,29 @@
 
         @pl.when(zi < line - 1)
         def _():
-            down_copy(zi, c).wait_recv()
+            down_copy(zi, c, True).wait_recv()
             part[zi, at] = part[zi, at] + going_down[zi, at]
 
         proj_ref[at] = (part[zi, at] + adapted[at]).astype(proj_ref.dtype)
         proj_out(c).start()
 
-    for copy in state_outs + adapter_outs:
+    sent(state, msem.at[0])
+    for copy in adapter_outs:
         copy.wait()
 
-    def sent(ref, sem):
-        pltpu.make_async_copy(ref, ref, sem).wait()
-
     sent(rbuf.at[pl.ds(0, n - 1)], rank_s.at[0])
-    sent(gsend, g_s.at[0])
+    tenant_copy.wait_send()
+    sent(raw_out, g_s.at[1])
+    low_copy.wait_send()
     sent(change.at[pl.ds(0, n - 1)], a_s.at[0])
-    sent(change.at[pl.ds(0, n - 1)], c_s.at[0])
+    sent(change.at[pl.ds(0, n - 2)], c_s.at[0])
+    sent(change.at[0, 0], h_s.at[0])
+    sent(scale_out, h_s.at[1])
+    sent(lent.at[0], l_s.at[0])
     sent(changes.at[pl.ds(0, n)], f_s.at[0])
     sent(ysend, y_s.at[0])
     sent(part.at[pl.ds(0, line - 1)], z_s.at[0])
-    for c in range(CHUNKS):
-        proj_out(c).wait()
+    sent(proj_ref, osem.at[2])
 
 
 def hand_out(*refs):
@@ -565,8 +674,8 @@
         scratch_shapes=[
             pltpu.SMEM((tenants,), jnp.int32),
             pltpu.VMEM((1, tokens), jnp.int32),
-            pltpu.VMEM((tokens, depth), bf16),
-            pltpu.VMEM((tokens, w), bf16),
+            pltpu.VMEM((1, tokens), jnp.int32),
+            pltpu.VMEM((2, 2 * tokens, w), bf16),
             pltpu.VMEM(adapter_down.shape, bf16),
             pltpu.VMEM(adapter_up.shape, bf16),
             pltpu.VMEM((tokens, w), bf16),
@@ -576,8 +685,10 @@
             pltpu.VMEM((4,) + momentum_down.shape, f32),
             pltpu.VMEM((2, lowrank, tokens), f32),
             pltpu.VMEM((n, 2, lowrank, tokens), f32),
-            pltpu.VMEM((2, n, lowrank, w), f32),
-            pltpu.VMEM((2, n, lowrank, w), f32),
+            pltpu.VMEM((2, tokens, w), f32),
+            pltpu.VMEM((2, tokens, w), f32),
+            pltpu.VMEM((2, lowrank, tokens), f32),
+            pltpu.VMEM((2, lowrank, tokens), f32),
             pltpu.VMEM((n, 2, lowrank, w), f32),
             pltpu.VMEM((n, 2, lowrank, w), f32),
             pltpu.VMEM((n, 2, lowrank, w), f32),
@@ -588,14 +699,17 @@
             pltpu.VMEM((line, tokens, w), f32),
             pltpu.VMEM((line, tokens, w), f32),
             pltpu.VMEM((tokens, w), f32),
+            pltpu.VMEM((2, 2, lowrank, w), f32),
+            pltpu.VMEM((8, 128), f32),
+            pltpu.VMEM((2, 8, 128), f32),
             dma((6,)),
-            dma((2 + CHUNKS,)),
+            dma((3,)),
             dma((n,)),
-            dma((4,)),
+            dma((1,)),
             dma((1,)),
             dma((n,)),
-            dma((1,)),
-            dma((2,)),
+            dma((3,)),
+            dma((4,)),
             dma((1,)),
             dma((n,)),
             dma((1,)),
@@ -605,8 +719,11 @@
             dma((1,)),
             dma((line * CHUNKS,)),
             dma((1,)),
-            dma((line * CHUNKS,)),
-            dma((line * CHUNKS,)),
+            dma(((line + 1) * CHUNKS,)),
+            dma((1,)),
+            dma((2,)),
+            dma((2,)),
+            dma((2,)),
         ],
         compiler_params=pltpu.CompilerParams(
             collective_id=0, has_side_effects=True, vmem_limit_bytes=48 * 1024 * 1024

time: 83.4 us -> 81.2 us (0.974)
  Pallas kernels: 82.5 us -> 80.4 us
    pallas_call x1, Pallas kernels: 80.7 us -> 78.6 us  [on_device(): pl.pallas_call(functools.partial(kernel, n), out_shape=(shape((tokens, w)...]
where the time goes in v3:
time: 81.2 us; the launch traced here: 81 us
  Pallas kernels  80.4 us (99%)
    pallas_call x1, Pallas kernels, on_device(): pl.pallas_call(functools.partial(kernel, n), out_shape=(shape((tokens, w)...  78.6 us
    pallas_call x1, Pallas kernels, on_device(): pl.pallas_call(hand_out, out_shape=tuple((shape(r.shape, r.dtype) for r i...  1.81 us

profile of v3, /device:TPU:9, one launch (start us, length us, event | category | flops | bytes accessed | tf_op | source)
XLA Modules:
  0.0 81.0 jit_solution(7955633135778915565)
XLA Ops:
  0.6 78.6 %shard_map.162 = (bf16[128,1024]{1,0:T(8,128)(2,1)S(1)}, bf16[16,16,1024]{2,1,0:T(8,128)(2,1)S(1)}, bf16[16,16,1024]{2,1,0:T(8,128)(2,1)S(1)}, f32[1,16,8192]{2,...) custom-call(s32[16]{0:T(128)} %owner_hbm.1, ...), custom_call_target="tpu_custom_call" | custom-call | tf_op jit(solution)/shard_map/pallas_call | solution.py:661
  79.2 1.8 %shard_map.163 = (bf16[128,1024]{1,0:T(8,128)(2,1)}, bf16[16,16,1024]{2,1,0:T(8,128)(2,1)}, bf16[16,16,1024]{2,1,0:T(8,128)(2,1)}, f32[1,16,8192]{2,1,0:T(8,128)...) custom-call(bf16[128,1024]{1,0:T(8,128)(2,1)S(1)} %get-tuple-element.14.refs_0_, ...), custom_call_target="tpu_custom_call" | custom-call | tf_op jit(solution)/shard_map/pallas_call | solution.py:749

commit v4 on v3

--- a/solution.py
+++ b/solution.py
@@ -20,7 +20,7 @@
 
 CHUNKS = 4
 EARLY = 1
-LEND_AT = 3
+LEND_AT = 1
 INNER = ((1, 0), (1, 1), (2, 0), (2, 1), (1, 2), (2, 2), (1, 3), (2, 3))
 
 
@@ -158,10 +158,10 @@
         for i, (src, dst) in enumerate(
             (
                 (tenant_hbm, tenant_ref),
+                (cot_hbm, cot_ref),
+                (up_hbm, up_ref),
                 (feat_hbm, feat_ref),
                 (down_hbm, down_ref),
-                (cot_hbm, cot_ref),
-                (up_hbm, up_ref),
                 (owner_hbm, owner_ref),
             )
         )
@@ -196,7 +196,10 @@
         ).reshape(tenants, lowrank, tokens)
         return jnp.sum(jnp.where(tenant_hit, scores, 0.0), axis=0)
 
-    for copy in in_copies[1:5]:
+    for copy in in_copies[1:3]:
+        copy.wait()
+    rpart[0] = rank_part(up_ref, cot_ref)
+    for copy in in_copies[3:]:
         copy.wait()
     for i, block in enumerate(blocks):
         weight_copy(i, block).start()
@@ -206,27 +209,27 @@
     ]
     for copy in state_copies:
         copy.start()
-    down_part = rank_part(down_ref, feat_ref)
-    up_part = rank_part(up_ref, cot_ref)
-    rpart[0] = down_part
-    rpart[1] = up_part
-    in_copies[5].wait()
-
     pl.semaphore_wait(barrier, n)
 
-    def rank_copy(o, source):
-        return pltpu.make_async_remote_copy(
-            src_ref=rpart,
-            dst_ref=rbuf.at[source],
+    def rank_copy(o, source, side):
+        return pltpu.make_async_remote_copy(
+            src_ref=rpart.at[side],
+            dst_ref=rbuf.at[side, source],
             send_sem=rank_s.at[0],
-            recv_sem=rank_r.at[source],
+            recv_sem=rank_r.at[side],
             device_id={"tensor": peer(o)},
             device_id_type=MESH,
         )
 
     @pl.loop(1, n)
     def _(o):
-        rank_copy(o, t).start()
+        rank_copy(o, t, 0).start()
+
+    rpart[1] = rank_part(down_ref, feat_ref)
+
+    @pl.loop(1, n)
+    def _(o):
+        rank_copy(o, t, 1).start()
 
     def mate_copy(source, target, out, arrived):
         return pltpu.make_async_remote_copy(
@@ -240,7 +243,7 @@
 
     tenant_copy = mate_copy(tenant_ref, mate_tenant, 0, 0)
     raw_copies = [mate_copy(raw_out.at[i], raw_in.at[i], 1, 1 + i) for i in range(2)]
-    low_copy = mate_copy(low_out, low_in, 2, 3)
+    low_copies = [mate_copy(low_out.at[i], low_in.at[i], 2 + i, 3 + i) for i in range(2)]
     tenant_copy.start()
     for i, rows in enumerate((feat_ref, cot_ref)):
         raw_out[i] = rows[...].astype(jnp.float32)
@@ -273,12 +276,12 @@
         for c in range(CHUNKS):
             pair_copy(z, c).start()
 
-    def frozen(i, block):
-        weight_copy(i, block).wait()
+    def frozen(i):
+        sent(wbuf.at[i], wsem.at[i])
         return jnp.dot(feat_ref[...], wbuf[i], preferred_element_type=jnp.float32)
 
     for i, z in enumerate(order):
-        ysend[z] = frozen(i, blocks[i])
+        ysend[z] = frozen(i)
         if i == 0:
             pair_start(z)
         if i == LEND_AT:
@@ -299,22 +302,6 @@
         raw_copies[i].wait_recv()
         rows_ref[i, tokens:] = raw_in[i].astype(jnp.bfloat16)
 
-    @pl.loop(1, n)
-    def _(o):
-        rank_copy(o, giver(o)).wait_recv()
-
-    rbuf[t] = rpart[...]
-    total = rbuf[0]
-    for source in range(1, n):
-        total = total + rbuf[source]
-    low = adapter_scale * total
-    down_low = low[0].astype(jnp.bfloat16).astype(jnp.float32)
-    up_low = low[1].astype(jnp.bfloat16).astype(jnp.float32)
-
-    low_out[0] = up_low
-    low_out[1] = down_low
-    low_copy.start()
-
     half_row = lax.broadcasted_iota(jnp.int32, (n, lowrank, tokens), 0) * 2 + d
 
     def spread(values, slot):
@@ -326,17 +313,26 @@
             src_ref=summed.at[peer(o), side],
             dst_ref=owned.at[source, side],
             send_sem=a_s.at[0],
-            recv_sem=a_r.at[source],
+            recv_sem=a_r.at[0],
             device_id={"tensor": peer(o)},
             device_id_type=MESH,
         )
 
-    both = pl.ds(0, 2)
-    own_part = [spread(low, slots[0]) for low in (up_low, down_low)]
-    low_copy.wait_recv()
+    lows = []
     for i in range(2):
+        sent(rbuf.at[i, pl.ds(0, n - 1)], rank_r.at[i])
+        rbuf[i, t] = rpart[i]
+        total = rbuf[i, 0]
+        for source in range(1, n):
+            total = total + rbuf[i, source]
+        low = (adapter_scale * total).astype(jnp.bfloat16).astype(jnp.float32)
+        low_out[i] = low
+        low_copies[i].start()
+        own_part = spread(low, slots[0])
+        lows.append(low)
+        low_copies[i].wait_recv()
         summed[:, i] = jnp.dot(
-            jnp.concatenate([own_part[i], spread(low_in[i], slots[1])], axis=1),
+            jnp.concatenate([own_part, spread(low_in[i], slots[1])], axis=1),
             rows_ref[i],
             preferred_element_type=jnp.float32,
         ).reshape(n, lowrank, w)
@@ -344,6 +340,8 @@
         @pl.loop(1, n)
         def _(o):
             grad_copy(o, t, i).start()
+
+    down_low = lows[1]
 
     pair_start(order[1])
 
@@ -356,7 +354,7 @@
         preferred_element_type=jnp.float32,
     )
     for i, z in enumerate(order):
-        part[z] = frozen(line + i, blocks[line + i])
+        part[z] = frozen(line + i)
 
     def up_copy(z, c):
         return pltpu.make_async_remote_copy(
@@ -425,9 +423,7 @@
 
     sent(state, msem.at[0])
 
-    @pl.loop(1, n)
-    def _(o):
-        grad_copy(o, giver(o), both).wait_recv()
+    sent(owned.at[pl.ds(0, n - 1)], a_r.at[0])
 
     def squares_of(k, acc):
         g = owned[k]
@@ -508,7 +504,7 @@
             src_ref=changes.at[at],
             dst_ref=changes.at[at],
             send_sem=f_s.at[0],
-            recv_sem=f_r.at[source],
+            recv_sem=f_r.at[0],
             device_id=mate,
             device_id_type=MESH,
         )
@@ -568,9 +564,7 @@
 
         forward_copy(source, d).start()
 
-    @pl.loop(0, n)
-    def _(source):
-        forward_copy(source, 1 - d).wait_recv()
+    sent(changes.at[pl.ds(0, n)], f_r.at[0])
 
     @pl.loop(0, tenants)
     def _(k):
@@ -610,10 +604,11 @@
     for copy in adapter_outs:
         copy.wait()
 
-    sent(rbuf.at[pl.ds(0, n - 1)], rank_s.at[0])
+    sent(rbuf.at[:, pl.ds(0, n - 1)], rank_s.at[0])
     tenant_copy.wait_send()
     sent(raw_out, g_s.at[1])
-    low_copy.wait_send()
+    for copy in low_copies:
+        copy.wait_send()
     sent(change.at[pl.ds(0, n - 1)], a_s.at[0])
     sent(change.at[pl.ds(0, n - 2)], c_s.at[0])
     sent(change.at[0, 0], h_s.at[0])
@@ -684,7 +679,7 @@
             pltpu.VMEM((n, depth, w), jnp.bfloat16),
             pltpu.VMEM((4,) + momentum_down.shape, f32),
             pltpu.VMEM((2, lowrank, tokens), f32),
-            pltpu.VMEM((n, 2, lowrank, tokens), f32),
+            pltpu.VMEM((2, n, lowrank, tokens), f32),
             pltpu.VMEM((2, tokens, w), f32),
             pltpu.VMEM((2, tokens, w), f32),
             pltpu.VMEM((2, lowrank, tokens), f32),
@@ -707,15 +702,15 @@
             dma((n,)),
             dma((1,)),
             dma((1,)),
+            dma((2,)),
+            dma((4,)),
+            dma((5,)),
+            dma((1,)),
+            dma((1,)),
+            dma((1,)),
             dma((n,)),
-            dma((3,)),
-            dma((4,)),
-            dma((1,)),
-            dma((n,)),
-            dma((1,)),
-            dma((n,)),
-            dma((1,)),
-            dma((n,)),
+            dma((1,)),
+            dma((1,)),
             dma((1,)),
             dma((line * CHUNKS,)),
             dma((1,)),

time: 81.2 us -> 81 us (level)
  no operation moved by 1% of the time
where the time goes in v4:
time: 81 us; the launch traced here: 80.7 us
  Pallas kernels  80.1 us (99%)
    pallas_call x1, Pallas kernels, on_device(): pl.pallas_call(functools.partial(kernel, n), out_shape=(shape((tokens, w)...  78.3 us
    pallas_call x1, Pallas kernels, on_device(): pl.pallas_call(hand_out, out_shape=tuple((shape(r.shape, r.dtype) for r i...  1.81 us

profile of v4, /device:TPU:9, one launch (start us, length us, event | category | flops | bytes accessed | tf_op | source)
XLA Modules:
  0.0 80.7 jit_solution(15547931894611071513)
XLA Ops:
  0.6 78.3 %shard_map.162 = (bf16[128,1024]{1,0:T(8,128)(2,1)S(1)}, bf16[16,16,1024]{2,1,0:T(8,128)(2,1)S(1)}, bf16[16,16,1024]{2,1,0:T(8,128)(2,1)S(1)}, f32[1,16,8192]{2,...) custom-call(s32[16]{0:T(128)} %owner_hbm.1, ...), custom_call_target="tpu_custom_call" | custom-call | tf_op jit(solution)/shard_map/pallas_call | solution.py:656
  78.9 1.8 %shard_map.163 = (bf16[128,1024]{1,0:T(8,128)(2,1)}, bf16[16,16,1024]{2,1,0:T(8,128)(2,1)}, bf16[16,16,1024]{2,1,0:T(8,128)(2,1)}, f32[1,16,8192]{2,1,0:T(8,128)...) custom-call(bf16[128,1024]{1,0:T(8,128)(2,1)S(1)} %get-tuple-element.14.refs_0_, ...), custom_call_target="tpu_custom_call" | custom-call | tf_op jit(solution)/shard_map/pallas_call | solution.py:744

commit v5 on v4

--- a/solution.py
+++ b/solution.py
@@ -272,8 +272,8 @@
             device_id_type=MESH,
         )
 
-    def pair_start(z):
-        for c in range(CHUNKS):
+    def pair_start(z, first=0, last=CHUNKS):
+        for c in range(first, last):
             pair_copy(z, c).start()
 
     def frozen(i):
@@ -283,7 +283,7 @@
     for i, z in enumerate(order):
         ysend[z] = frozen(i)
         if i == 0:
-            pair_start(z)
+            pair_start(z, 0, 2)
         if i == LEND_AT:
             for k in range(2):
                 lent_copy(k).start()
@@ -343,6 +343,7 @@
 
     down_low = lows[1]
 
+    pair_start(order[0], 2)
     pair_start(order[1])
 
     owned[t] = summed[t]

time: 81 us -> 81 us (level)
  no operation moved by 1% of the time
where the time goes in v5:
time: 81 us; the launch traced here: 80.7 us
  Pallas kernels  80.1 us (99%)
    pallas_call x1, Pallas kernels, on_device(): pl.pallas_call(functools.partial(kernel, n), out_shape=(shape((tokens, w)...  78.3 us
    pallas_call x1, Pallas kernels, on_device(): pl.pallas_call(hand_out, out_shape=tuple((shape(r.shape, r.dtype) for r i...  1.81 us

profile of v5, /device:TPU:9, one launch (start us, length us, event | category | flops | bytes accessed | tf_op | source)
XLA Modules:
  0.0 80.7 jit_solution(9583435873296848390)
XLA Ops:
  0.6 78.3 %shard_map.162 = (bf16[128,1024]{1,0:T(8,128)(2,1)S(1)}, bf16[16,16,1024]{2,1,0:T(8,128)(2,1)S(1)}, bf16[16,16,1024]{2,1,0:T(8,128)(2,1)S(1)}, f32[1,16,8192]{2,...) custom-call(s32[16]{0:T(128)} %owner_hbm.1, ...), custom_call_target="tpu_custom_call" | custom-call | tf_op jit(solution)/shard_map/pallas_call | solution.py:657
  78.9 1.8 %shard_map.163 = (bf16[128,1024]{1,0:T(8,128)(2,1)}, bf16[16,16,1024]{2,1,0:T(8,128)(2,1)}, bf16[16,16,1024]{2,1,0:T(8,128)(2,1)}, f32[1,16,8192]{2,1,0:T(8,128)...) custom-call(bf16[128,1024]{1,0:T(8,128)(2,1)S(1)} %get-tuple-element.14.refs_0_, ...), custom_call_target="tpu_custom_call" | custom-call | tf_op jit(solution)/shard_map/pallas_call | solution.py:745

commit v6 on v5

--- a/solution.py
+++ b/solution.py
@@ -20,7 +20,7 @@
 
 CHUNKS = 4
 EARLY = 1
-LEND_AT = 1
+LEND_AT = 0
 INNER = ((1, 0), (1, 1), (2, 0), (2, 1), (1, 2), (2, 2), (1, 3), (2, 3))
 
 

time: 81 us -> 81 us (level)
  no operation moved by 1% of the time
where the time goes in v6:
time: 81 us; the launch traced here: 80.7 us
  Pallas kernels  80.1 us (99%)
    pallas_call x1, Pallas kernels, on_device(): pl.pallas_call(functools.partial(kernel, n), out_shape=(shape((tokens, w)...  78.3 us
    pallas_call x1, Pallas kernels, on_device(): pl.pallas_call(hand_out, out_shape=tuple((shape(r.shape, r.dtype) for r i...  1.81 us

profile of v6, /device:TPU:9, one launch (start us, length us, event | category | flops | bytes accessed | tf_op | source)
XLA Modules:
  0.0 80.7 jit_solution(15513831819683859573)
XLA Ops:
  0.6 78.3 %shard_map.162 = (bf16[128,1024]{1,0:T(8,128)(2,1)S(1)}, bf16[16,16,1024]{2,1,0:T(8,128)(2,1)S(1)}, bf16[16,16,1024]{2,1,0:T(8,128)(2,1)S(1)}, f32[1,16,8192]{2,...) custom-call(s32[16]{0:T(128)} %owner_hbm.1, ...), custom_call_target="tpu_custom_call" | custom-call | tf_op jit(solution)/shard_map/pallas_call | solution.py:657
  78.9 1.8 %shard_map.163 = (bf16[128,1024]{1,0:T(8,128)(2,1)}, bf16[16,16,1024]{2,1,0:T(8,128)(2,1)}, bf16[16,16,1024]{2,1,0:T(8,128)(2,1)}, f32[1,16,8192]{2,1,0:T(8,128)...) custom-call(bf16[128,1024]{1,0:T(8,128)(2,1)S(1)} %get-tuple-element.14.refs_0_, ...), custom_call_target="tpu_custom_call" | custom-call | tf_op jit(solution)/shard_map/pallas_call | solution.py:745
